TPU v7x, 32 devices: a whole 2x2x4 slice. The times are simulated.
32 devices in a mesh: dp: 8 (over z, x), mp: 4 (over y, core).
Axes of the slice: x: 2, y: 2, z: 4, core: 2. Of those that a mesh axis runs over, the one named last changes fastest.
Arguments:
- tokens: bfloat16 [8192, 2048], P(('dp', 'mp')), may hold values from -6 to 6
- cotangent: bfloat16 [8192, 2048], P(('dp', 'mp')), as said below
- gains_master: float32 [2, 2048], replicated, may hold values from 0.5 to 1.5
- scoring_master: float32 [2, 2048, 2048], P(None, 'dp', 'mp'), as said below
- mixing_master: float32 [2, 2048, 4096], P(None, 'dp', 'mp'), as said below
- output_master: float32 [4096, 2048], P(('mp', 'dp')), as said below
- expand_master: float32 [2048, 4096], P('dp', 'mp'), as said below
- shrink_master: float32 [4096, 2048], P(('mp', 'dp')), as said below
- gains_first: float32 [2, 2048], replicated, may hold values from -64 to 64
- gains_second: float32 [2, 2048], replicated, may hold values from 4.096 to 32.768
- scoring_first: float32 [2, 2048, 2048], P(None, 'dp', 'mp'), may hold values from -64 to 64
- scoring_second: float32 [2, 2048, 2048], P(None, 'dp', 'mp'), as said below
- mixing_first: float32 [2, 2048, 4096], P(None, 'dp', 'mp'), may hold values from -28 to 28
- mixing_second: float32 [2, 2048, 4096], P(None, 'dp', 'mp'), as said below
- output_first: float32 [4096, 2048], P(('mp', 'dp')), may hold values from -40 to 40
- output_second: float32 [4096, 2048], P(('mp', 'dp')), as said below
- expand_first: float32 [2048, 4096], P('dp', 'mp'), may hold values from -20 to 20
- expand_second: float32 [2048, 4096], P('dp', 'mp'), as said below
- shrink_first: float32 [4096, 2048], P(('mp', 'dp')), may hold values from -32 to 32
- shrink_second: float32 [4096, 2048], P(('mp', 'dp')), as said below
Outputs:
- layer_output: bfloat16 [8192, 2048], P(('dp', 'mp'))
- input_grad: float32 [8192, 2048], P(('dp', 'mp'))
- gains_grad: float32 [2, 2048], replicated
- scoring_grad: float32 [2, 2048, 2048], P(None, 'dp', 'mp')
- mixing_grad: float32 [2, 2048, 4096], P(None, 'dp', 'mp')
- output_grad: float32 [4096, 2048], P(('mp', 'dp'))
- expand_grad: float32 [2048, 4096], P('dp', 'mp')
- shrink_grad: float32 [4096, 2048], P(('mp', 'dp'))
- gains_moment: float32 [2, 2048], replicated
- scoring_moment: float32 [2, 2048, 2048], P(None, 'dp', 'mp')
- mixing_moment: float32 [2, 2048, 4096], P(None, 'dp', 'mp')
- output_moment: float32 [4096, 2048], P(('mp', 'dp'))
- expand_moment: float32 [2048, 4096], P('dp', 'mp')
- shrink_moment: float32 [4096, 2048], P(('mp', 'dp'))
- gains_square: float32 [2, 2048], replicated
- scoring_square: float32 [2, 2048, 2048], P(None, 'dp', 'mp')
- mixing_square: float32 [2, 2048, 4096], P(None, 'dp', 'mp')
- output_square: float32 [4096, 2048], P(('mp', 'dp'))
- expand_square: float32 [2048, 4096], P('dp', 'mp')
- shrink_square: float32 [4096, 2048], P(('mp', 'dp'))
- gains_weight: float32 [2, 2048], replicated
- scoring_weight: float32 [2, 2048, 2048], P(None, 'dp', 'mp')
- mixing_weight: float32 [2, 2048, 4096], P(None, 'dp', 'mp')
- output_weight: float32 [4096, 2048], P(('mp', 'dp'))
- expand_weight: float32 [2048, 4096], P('dp', 'mp')
- shrink_weight: float32 [4096, 2048], P(('mp', 'dp'))
- scoring_copy: bfloat16 [2, 2048, 2048], P(None, 'dp', 'mp')
- mixing_copy: bfloat16 [2, 2048, 4096], P(None, 'dp', 'mp')
- output_copy: bfloat16 [4096, 2048], P(('mp', 'dp'))
- expand_copy: bfloat16 [2048, 4096], P('dp', 'mp')
- shrink_copy: bfloat16 [4096, 2048], P(('mp', 'dp'))
- trust_norms: float32 [2, 9], replicated
Inputs may be any that keep to these rules, and one draw needn't show every extreme that they name: `cotangent`: entries of either sign. `scoring_master`: entries of either sign. `mixing_master`: entries of either sign. `output_master`: entries of either sign. `expand_master`: entries of either sign. `shrink_master`: entries of either sign. `scoring_second`: positive entries. `mixing_second`: positive entries. `output_second`: positive entries. `expand_second`: positive entries. `shrink_second`: positive entries.
All inputs are finite; a program needn't handle non-finite values.
Results may differ from a plain program's by a relative error of at most 0.017.
The roundings to bfloat16 on the way count: a program that leaves them out, or rounds other values in their place, can miss the bound.
Values may be sent and summed in bfloat16 or wider, within the bound.
A program may use at most 256 MiB of HBM per device.

v0:
```python
import jax
import jax.numpy as jnp
from jax import lax
from jax.sharding import PartitionSpec as P

DK = 256
DV = 512
beta_one = 0.9
beta_two = 0.999
lamb_epsilon = 1e-06
decay_rate = 0.01
learn_rate = 0.5
norm_epsilon = 1e-06


def rms_scale(values, gain_row):
    return (
        values
        * lax.rsqrt(jnp.mean(values * values, axis=-1, keepdims=True) + norm_epsilon)
        * gain_row
    )


def rotate(values, direction):
    length, heads, features = values.shape
    half = features // 2
    freqs = 10000.0 ** (-jnp.linspace(0.0, 1.0, half, dtype=jnp.float32))
    angle = jnp.arange(length, dtype=jnp.float32)[:, None] * freqs[None, :]
    cosine = jnp.cos(angle)[:, None, :]
    sine = direction * jnp.sin(angle)[:, None, :]
    pairs = values.reshape(length, heads, half, 2)
    even = pairs[..., 0]
    oddly = pairs[..., 1]
    turned = jnp.stack((even * cosine - oddly * sine, oddly * cosine + even * sine), axis=-1)
    return turned.reshape(length, heads, features)


def decay_table(offset, rows_count, length, decay_logs):
    row_pos = offset + jnp.arange(rows_count, dtype=jnp.int32)
    col_pos = jnp.arange(length, dtype=jnp.int32)
    spacing = (row_pos[:, None] - col_pos[None, :]).astype(jnp.float32)
    return jnp.where(
        spacing >= 0.0, jnp.exp(decay_logs[:, None, None] * jnp.maximum(spacing, 0.0)), 0.0
    )


def gate_norm(retained, gate_pre):
    normal = retained * lax.rsqrt(
        jnp.mean(retained * retained, axis=-1, keepdims=True) + norm_epsilon
    )
    return jax.nn.silu(gate_pre) * normal


def gelu_exact(values):
    return jax.nn.gelu(values, approximate=False)


def contract_rows(left, right):
    return lax.dot_general(
        left, right, (((0,), (0,)), ((), ())), preferred_element_type=jnp.float32
    )


def contract_cols(left, right):
    return lax.dot_general(
        left, right, (((1,), (1,)), ((), ())), preferred_element_type=jnp.float32
    )


def retention_forward(turned_queries, turned_keys, values, decay_logs, block_rows):
    length = turned_keys.shape[0]

    def one_block(block_index):
        offset = block_index * block_rows
        query_part = lax.dynamic_slice_in_dim(turned_queries, offset, block_rows, 0)
        scores = jnp.einsum(
            "qhd,khd->hqk", query_part, turned_keys, preferred_element_type=jnp.float32
        )
        weights = (scores * decay_table(offset, block_rows, length, decay_logs)).astype(
            jnp.bfloat16
        )
        retained = jnp.einsum("hqk,khe->qhe", weights, values, preferred_element_type=jnp.float32)
        return (retained, weights)

    retained_blocks, weight_blocks = lax.map(one_block, jnp.arange(length // block_rows))
    return (retained_blocks.reshape(length, values.shape[1], values.shape[2]), weight_blocks)


def retention_backward(turned_queries, turned_keys, values, retained_low, decay_logs, block_rows):
    length = turned_keys.shape[0]

    def one_block(totals, block_index):
        offset = block_index * block_rows
        query_part = lax.dynamic_slice_in_dim(turned_queries, offset, block_rows, 0)
        back_part = lax.dynamic_slice_in_dim(retained_low, offset, block_rows, 0)
        table = decay_table(offset, block_rows, length, decay_logs)
        scores = jnp.einsum(
            "qhd,khd->hqk", query_part, turned_keys, preferred_element_type=jnp.float32
        )
        weights = (scores * table).astype(jnp.bfloat16)
        weight_back = jnp.einsum(
            "qhe,khe->hqk", back_part, values, preferred_element_type=jnp.float32
        )
        score_back = (weight_back * table).astype(jnp.bfloat16)
        query_grad = jnp.einsum(
            "hqk,khd->qhd", score_back, turned_keys, preferred_element_type=jnp.float32
        )
        keys_total = totals[0] + jnp.einsum(
            "hqk,qhd->khd", score_back, query_part, preferred_element_type=jnp.float32
        )
        values_total = totals[1] + jnp.einsum(
            "hqk,qhe->khe", weights, back_part, preferred_element_type=jnp.float32
        )
        return ((keys_total, values_total), query_grad)

    start_totals = (jnp.zeros(turned_keys.shape, jnp.float32), jnp.zeros(values.shape, jnp.float32))
    (keys_grad, values_grad), query_blocks = lax.scan(
        one_block, start_totals, jnp.arange(length // block_rows)
    )
    return (query_blocks.reshape(turned_queries.shape), keys_grad, values_grad)


def lamb_parts(weight, grad, first, second):
    moment = beta_one * first + (1.0 - beta_one) * grad
    square = beta_two * second + (1.0 - beta_two) * grad * grad
    update = moment / (jnp.sqrt(square) + lamb_epsilon) + decay_rate * weight
    return (moment, square, update)


def body(
    tokens,
    cotangent,
    gains_master,
    scoring_master,
    mixing_master,
    output_master,
    expand_master,
    shrink_master,
    gains_first,
    gains_second,
    scoring_first,
    scoring_second,
    mixing_first,
    mixing_second,
    output_first,
    output_second,
    expand_first,
    expand_second,
    shrink_first,
    shrink_second,
):
    scoring_low, mixing_low, output_low, expand_low, shrink_low = (
        lax.all_gather(scoring_master.astype(jnp.bfloat16), "dp", axis=1, tiled=True),
        lax.all_gather(mixing_master.astype(jnp.bfloat16), "dp", axis=1, tiled=True),
        lax.all_gather(output_master.astype(jnp.bfloat16), "dp", axis=0, tiled=True),
        lax.all_gather(expand_master.astype(jnp.bfloat16), "dp", axis=0, tiled=True),
        lax.all_gather(shrink_master.astype(jnp.bfloat16), "dp", axis=0, tiled=True),
    )
    model_devices = lax.axis_size("mp")
    local_rows = tokens.shape[0]
    length = local_rows * model_devices
    heads_local = scoring_low.shape[2] // DK
    head_start = lax.axis_index("mp") * heads_local
    decay_logs = jnp.log(
        1.0
        - 2.0
        ** (-5.0 - (head_start + jnp.arange(heads_local, dtype=jnp.int32)).astype(jnp.float32))
    )
    block_rows = min(512, length)
    inputs = tokens.astype(jnp.float32)
    gain_one = gains_master[0]
    gain_two = gains_master[1]
    normed = rms_scale(inputs, gain_one).astype(jnp.bfloat16)
    normed_all = lax.all_gather(normed, "mp", axis=0, tiled=True)
    queries = jnp.dot(normed_all, scoring_low[0], preferred_element_type=jnp.float32)
    keys_pre = jnp.dot(normed_all, scoring_low[1], preferred_element_type=jnp.float32)
    values = (
        jnp.dot(normed_all, mixing_low[0], preferred_element_type=jnp.float32)
        .astype(jnp.bfloat16)
        .reshape(length, heads_local, DV)
    )
    gate_pre = jnp.dot(normed_all, mixing_low[1], preferred_element_type=jnp.float32).reshape(
        length, heads_local, DV
    )
    turned_queries = rotate(queries.reshape(length, heads_local, DK), 1.0).astype(jnp.bfloat16)
    turned_keys = rotate(keys_pre.reshape(length, heads_local, DK), 1.0).astype(jnp.bfloat16)
    retained, weight_blocks = retention_forward(
        turned_queries, turned_keys, values, decay_logs, block_rows
    )
    mixed_rows = (
        gate_norm(retained, gate_pre).reshape(length, heads_local * DV).astype(jnp.bfloat16)
    )
    branch = lax.psum_scatter(
        jnp.dot(mixed_rows, output_low, preferred_element_type=jnp.float32),
        "mp",
        scatter_dimension=0,
        tiled=True,
    )
    hidden = inputs + branch
    second_in = rms_scale(hidden, gain_two).astype(jnp.bfloat16)
    second_all = lax.all_gather(second_in, "mp", axis=0, tiled=True)
    upward = jnp.dot(second_all, expand_low, preferred_element_type=jnp.float32)
    active = gelu_exact(upward).astype(jnp.bfloat16)
    ffn_branch = lax.psum_scatter(
        jnp.dot(active, shrink_low, preferred_element_type=jnp.float32),
        "mp",
        scatter_dimension=0,
        tiled=True,
    )
    layer_output = (hidden + ffn_branch).astype(jnp.bfloat16)
    back_all = lax.all_gather(cotangent, "mp", axis=0, tiled=True)
    shrink_local = contract_rows(active, back_all)
    active_back = contract_cols(back_all, shrink_low)
    gelu_pull = jax.vjp(gelu_exact, upward)[1]
    upward_back = gelu_pull(active_back)[0].astype(jnp.bfloat16)
    expand_local = contract_rows(second_all, upward_back)
    second_back = lax.psum_scatter(
        contract_cols(upward_back, expand_low), "mp", scatter_dimension=0, tiled=True
    )
    norm_two_pull = jax.vjp(rms_scale, hidden, gain_two)[1]
    hidden_part, gain_two_grad = norm_two_pull(second_back)
    hidden_back = cotangent.astype(jnp.float32) + hidden_part
    branch_back = hidden_back.astype(jnp.bfloat16)
    branch_all = lax.all_gather(branch_back, "mp", axis=0, tiled=True)
    output_local = contract_rows(mixed_rows, branch_all)
    mixed_back = contract_cols(branch_all, output_low)
    gate_pull = jax.vjp(gate_norm, retained, gate_pre)[1]
    retained_back, gate_back = gate_pull(mixed_back.reshape(length, heads_local, DV))
    retained_low = retained_back.astype(jnp.bfloat16)
    gate_low = gate_back.astype(jnp.bfloat16).reshape(length, heads_local * DV)
    turned_query_back, turned_key_back, values_back = retention_backward(
        turned_queries, turned_keys, values, retained_low, decay_logs, block_rows
    )
    query_low = (
        rotate(turned_query_back, -1.0).astype(jnp.bfloat16).reshape(length, heads_local * DK)
    )
    keys_low = rotate(turned_key_back, -1.0).astype(jnp.bfloat16).reshape(length, heads_local * DK)
    values_low = values_back.astype(jnp.bfloat16).reshape(length, heads_local * DV)
    scoring_local = jnp.stack(
        (contract_rows(normed_all, query_low), contract_rows(normed_all, keys_low))
    )
    mixing_local = jnp.stack(
        (contract_rows(normed_all, values_low), contract_rows(normed_all, gate_low))
    )
    total = contract_cols(query_low, scoring_low[0])
    total = total + contract_cols(keys_low, scoring_low[1])
    total = total + contract_cols(values_low, mixing_low[0])
    normed_back = lax.psum_scatter(
        total + contract_cols(gate_low, mixing_low[1]), "mp", scatter_dimension=0, tiled=True
    )
    norm_one_pull = jax.vjp(rms_scale, inputs, gain_one)[1]
    inputs_part, gain_one_grad = norm_one_pull(normed_back)
    input_grad = hidden_back + inputs_part
    scoring_grad, mixing_grad, output_grad, expand_grad, shrink_grad = (
        lax.psum_scatter(scoring_local, "dp", scatter_dimension=1, tiled=True),
        lax.psum_scatter(mixing_local, "dp", scatter_dimension=1, tiled=True),
        lax.psum_scatter(output_local, "dp", scatter_dimension=0, tiled=True),
        lax.psum_scatter(expand_local, "dp", scatter_dimension=0, tiled=True),
        lax.psum_scatter(shrink_local, "dp", scatter_dimension=0, tiled=True),
    )
    gains_grad = lax.psum(jnp.stack((gain_one_grad, gain_two_grad)), ("dp", "mp"))
    scoring_moment, scoring_square, scoring_update = lamb_parts(
        scoring_master, scoring_grad, scoring_first, scoring_second
    )
    mixing_moment, mixing_square, mixing_update = lamb_parts(
        mixing_master, mixing_grad, mixing_first, mixing_second
    )
    output_moment, output_square, output_update = lamb_parts(
        output_master, output_grad, output_first, output_second
    )
    expand_moment, expand_square, expand_update = lamb_parts(
        expand_master, expand_grad, expand_first, expand_second
    )
    shrink_moment, shrink_square, shrink_update = lamb_parts(
        shrink_master, shrink_grad, shrink_first, shrink_second
    )
    gains_moment, gains_square, gains_update = lamb_parts(
        gains_master, gains_grad, gains_first, gains_second
    )
    weight_local = jnp.concatenate(
        (
            jnp.sum(scoring_master * scoring_master, axis=(1, 2)),
            jnp.sum(mixing_master * mixing_master, axis=(1, 2)),
            jnp.stack(
                (
                    jnp.sum(output_master * output_master),
                    jnp.sum(expand_master * expand_master),
                    jnp.sum(shrink_master * shrink_master),
                )
            ),
        )
    )
    update_local = jnp.concatenate(
        (
            jnp.sum(scoring_update * scoring_update, axis=(1, 2)),
            jnp.sum(mixing_update * mixing_update, axis=(1, 2)),
            jnp.stack(
                (
                    jnp.sum(output_update * output_update),
                    jnp.sum(expand_update * expand_update),
                    jnp.sum(shrink_update * shrink_update),
                )
            ),
        )
    )
    weight_total, update_total = lax.psum((weight_local, update_local), ("dp", "mp"))
    weight_norms = jnp.sqrt(weight_total)
    update_norms = jnp.sqrt(update_total)
    ratios = weight_norms / update_norms
    gains_wnorm = jnp.sqrt(jnp.sum(gains_master * gains_master, axis=1))
    gains_unorm = jnp.sqrt(jnp.sum(gains_update * gains_update, axis=1))
    scoring_weight = scoring_master - learn_rate * ratios[0:2][:, None, None] * scoring_update
    mixing_weight = mixing_master - learn_rate * ratios[2:4][:, None, None] * mixing_update
    output_weight = output_master - learn_rate * ratios[4] * output_update
    expand_weight = expand_master - learn_rate * ratios[5] * expand_update
    shrink_weight = shrink_master - learn_rate * ratios[6] * shrink_update
    gains_weight = gains_master - learn_rate * (gains_wnorm / gains_unorm)[:, None] * gains_update
    trust_norms = jnp.stack(
        (jnp.concatenate((weight_norms, gains_wnorm)), jnp.concatenate((update_norms, gains_unorm)))
    )
    return (
        layer_output,
        input_grad,
        gains_grad,
        scoring_grad,
        mixing_grad,
        output_grad,
        expand_grad,
        shrink_grad,
        gains_moment,
        scoring_moment,
        mixing_moment,
        output_moment,
        expand_moment,
        shrink_moment,
        gains_square,
        scoring_square,
        mixing_square,
        output_square,
        expand_square,
        shrink_square,
        gains_weight,
        scoring_weight,
        mixing_weight,
        output_weight,
        expand_weight,
        shrink_weight,
        scoring_weight.astype(jnp.bfloat16),
        mixing_weight.astype(jnp.bfloat16),
        output_weight.astype(jnp.bfloat16),
        expand_weight.astype(jnp.bfloat16),
        shrink_weight.astype(jnp.bfloat16),
        trust_norms,
    )


def solution(mesh):
    placed = (
        P(("dp", "mp"), None),
        P(("dp", "mp"), None),
        P(),
        P(None, "dp", "mp"),
        P(None, "dp", "mp"),
        P(("mp", "dp"), None),
        P("dp", "mp"),
        P(("mp", "dp"), None),
        P(),
        P(),
        P(None, "dp", "mp"),
        P(None, "dp", "mp"),
        P(None, "dp", "mp"),
        P(None, "dp", "mp"),
        P(("mp", "dp"), None),
        P(("mp", "dp"), None),
        P("dp", "mp"),
        P("dp", "mp"),
        P(("mp", "dp"), None),
        P(("mp", "dp"), None),
    )
    return jax.shard_map(
        body,
        mesh=mesh,
        in_specs=placed,
        out_specs=(
            P(("dp", "mp"), None),
            P(("dp", "mp"), None),
            P(),
            P(None, "dp", "mp"),
            P(None, "dp", "mp"),
            P(("mp", "dp"), None),
            P("dp", "mp"),
            P(("mp", "dp"), None),
            P(),
            P(None, "dp", "mp"),
            P(None, "dp", "mp"),
            P(("mp", "dp"), None),
            P("dp", "mp"),
            P(("mp", "dp"), None),
            P(),
            P(None, "dp", "mp"),
            P(None, "dp", "mp"),
            P(("mp", "dp"), None),
            P("dp", "mp"),
            P(("mp", "dp"), None),
            P(),
            P(None, "dp", "mp"),
            P(None, "dp", "mp"),
            P(("mp", "dp"), None),
            P("dp", "mp"),
            P(("mp", "dp"), None),
            P(None, "dp", "mp"),
            P(None, "dp", "mp"),
            P(("mp", "dp"), None),
            P("dp", "mp"),
            P(("mp", "dp"), None),
            P(),
        ),
        check_vma=False,
    )
```

profile of v0, /device:TPU:0, one launch (start us, length us, event | category | flops | bytes accessed | tf_op | source)
XLA Modules:
  0.0 1868.9 jit_solution(18121619089342116246)
XLA Ops:
  21.0 65.3 %all-gather.14.cloned.1.call-done = bf16[2,2048,512]{2,1,0:T(8,128)(2,1)} async-done(((bf16[2,256,512]{2,1,0:T(8,128)(2,1)}), bf16[2,2048,512]{2,1,0:T(8,128)(2,1)}) %all-gather.14.cloned.1.call-update) | async-done | bytes 4194320 | tf_op jit(solution)/shard_map/all_gather | solution.py:153
  102.0 19.4 %all-gather.10.cloned.1.call-done = bf16[1024,2048]{1,0:T(8,128)(2,1)} async-done(((bf16[256,2048]{1,0:T(8,128)(2,1)}), bf16[1024,2048]{1,0:T(8,128)(2,1)}) %all-gather.10.cloned.1.call-update) | async-done | bytes 4194320 | tf_op jit(solution)/shard_map/all_gather | solution.py:174
  121.5 5.4 fusion.20
  135.9 112.8 %all-gather.12.cloned.1.call-done = bf16[2,2048,1024]{2,1,0:T(8,128)(2,1)} async-done(((bf16[2,256,1024]{2,1,0:T(8,128)(2,1)}), bf16[2,2048,1024]{2,1,0:T(8,128)(2,1)}) %all-gather.12.cloned.1.call-update) | async-done | bytes 8388624 | tf_op jit(solution)/shard_map/all_gather | solution.py:154
  248.7 8.0 fusion.51
  264.0 6.5 copy.86
  270.5 18.0 while.26
  273.9 5.4 bitcast_dynamic-update-slice_fusion.2
  282.8 5.7 bitcast_dynamic-update-slice_fusion.2
  288.5 7.3 copy.96
  295.8 7.0 reshape.309
  306.3 10.5 multiply_convert_fusion.4
  316.8 5.5 all-gather.16.cloned.1.call-done
  322.3 8.9 fusion.83
  333.4 68.0 %reduce-scatter.10.cloned.1.call-done = f32[256,2048]{1,0:T(8,128)} async-done(((f32[1024,2048]{1,0:T(8,128)}), f32[256,2048]{1,0:T(8,128)}) %reduce-scatter.10.cloned.1.call-update) | async-done | bytes 2097168 | tf_op jit(solution)/shard_map/reduce_scatter | solution.py:193
  407.8 68.9 %all-gather.20.cloned.1.call-done = bf16[2048,1024]{1,0:T(8,128)(2,1)} async-done(((bf16[256,1024]{1,0:T(8,128)(2,1)}), bf16[2048,1024]{1,0:T(8,128)(2,1)}) %all-gather.20.cloned.1.call-update) | async-done | bytes 4194320 | tf_op jit(solution)/shard_map/all_gather | solution.py:156
  476.7 35.2 %all-gather.18.cloned.1.call-done = bf16[1024,2048]{1,0:T(8,128)(2,1)} async-done(((bf16[256,2048]{1,0:T(8,128)(2,1)}), bf16[1024,2048]{1,0:T(8,128)(2,1)}) %all-gather.18.cloned.1.call-update) | async-done | bytes 4194320 | tf_op jit(solution)/shard_map/all_gather | solution.py:201
  511.9 9.9 fusion.84
  521.8 26.1 %all-gather.24.cloned.1.call-done = bf16[1024,2048]{1,0:T(8,128)(2,1)} async-done(((bf16[256,2048]{1,0:T(8,128)(2,1)}), bf16[1024,2048]{1,0:T(8,128)(2,1)}) %all-gather.24.cloned.1.call-update) | async-done | bytes 4194320 | tf_op jit(solution)/shard_map/all_gather | solution.py:211
  547.9 75.5 %all-gather.22.cloned.1.call-done = bf16[1024,2048]{1,0:T(8,128)(2,1)} async-done(((bf16[128,2048]{1,0:T(8,128)(2,1)}), bf16[1024,2048]{1,0:T(8,128)(2,1)}) %all-gather.22.cloned.1.call-update) | async-done | bytes 4194320 | tf_op jit(solution)/shard_map/all_gather | solution.py:157
  623.5 18.9 %add_convert_fusion = (bf16[1024,1024]{1,0:T(8,128)(2,1)S(1)}, f32[1024,1024]{1,0:T(8,128)}) fusion(f32[1024,1024]{1,0:T(8,128)} %fusion.84, bf16[1024,2048]{1,0:T(8,128)(2,1)} %all-gather.24.cloned.1.call-done, bf16[1024,2048]{1,0:T(8,128)(2,1)} %all-gather.22.cloned.1.call-done), kind=kOutput, calls=%fused_computation.54 | convolution fusion | flops 4370464768 | bytes 18874368 | tf_op jit(solution)/shard_map/dot_general | solution.py:65
  643.6 6.8 fusion.86
  650.5 70.1 %reduce-scatter.14.cloned.1.call-done = f32[256,2048]{1,0:T(8,128)} async-done(((f32[1024,2048]{1,0:T(8,128)}), f32[256,2048]{1,0:T(8,128)}) %reduce-scatter.14.cloned.1.call-update) | async-done | bytes 2097168 | tf_op jit(solution)/shard_map/reduce_scatter | solution.py:217
  731.9 7.1 fusion.89
  740.7 9.0 fusion.88
  749.8 10.6 all-gather.26.cloned.1.call-done
  760.4 11.1 multiply_reduce_fusion
  776.0 81.4 %while.27 = (s32[]{:T(128)}, f32[1024,2,256]{0,2,1:T(8,128)}, f32[1024,2,512]{0,2,1:T(8,128)}, f32[2,512,2,256]{1,0,3,2:T(2,128)}, s32[2]{0:T(128)S(1)}, /*index...) while((s32[]{:T(128)}, f32[1024,2,256]{0,2,1:T(8,128)}, ...), condition=%wide.region_11.13_spmd.clone, body=%wide.region_10.12_spmd.clone.sunk | while | flops 3772776960 | bytes 48765212 | solution.py:117
  788.9 6.8 bitcast_add_fusion.5
  795.7 19.6 %dynamic_update_slice.14 = f32[2,512,2,256]{1,0,3,2:T(2,128)} dynamic-update-slice(f32[2,512,2,256]{1,0,3,2:T(2,128)} %get-tuple-element.510, f32[1,512,2,256]{1,0,3,2:T(1,128)S(1)} %copy.168, s32[]{:T(128)S(6)} %copy.181, s32[]{:T(128)} %constant.79.clone.1..sunk.1, s32[]{:T(128)} %constant.79.clone.1..sunk.1, s32[]{:T(128)} %constant.79.clone.1..sunk.1) | dynamic-update-slice | bytes 2097156 | tf_op jit(solution)/shard_map/while/body/jit(dynamic_update_index_in_dim)/dynamic_update_slice | solution.py:117
  829.8 8.0 bitcast_add_fusion.5
  837.8 19.6 %dynamic_update_slice.14 = f32[2,512,2,256]{1,0,3,2:T(2,128)} dynamic-update-slice(f32[2,512,2,256]{1,0,3,2:T(2,128)} %get-tuple-element.510, f32[1,512,2,256]{1,0,3,2:T(1,128)S(1)} %copy.168, s32[]{:T(128)S(6)} %copy.181, s32[]{:T(128)} %constant.79.clone.1..sunk.1, s32[]{:T(128)} %constant.79.clone.1..sunk.1, s32[]{:T(128)} %constant.79.clone.1..sunk.1) | dynamic-update-slice | bytes 2097156 | tf_op jit(solution)/shard_map/while/body/jit(dynamic_update_index_in_dim)/dynamic_update_slice | solution.py:117
  878.3 9.8 fusion.24
  888.1 6.9 fusion.34
  895.0 12.3 add_add_fusion
  907.3 10.6 fusion.87
  931.3 8.9 fusion.85
  940.3 7.2 convolution_bitcast_fusion.2
  952.3 6.4 pad_maximum_fusion
  964.7 98.1 %reduce-scatter.24.cloned.1.call-done = f32[256,1024]{1,0:T(8,128)} async-done(((f32[2048,1024]{1,0:T(8,128)}), f32[256,1024]{1,0:T(8,128)}) %reduce-scatter.24.cloned.1.call-update) | async-done | bytes 1048592 | tf_op jit(solution)/shard_map/reduce_scatter | solution.py:258
  1067.3 68.4 %reduce-scatter.16.cloned.1.call-done = f32[256,2048]{1,0:T(8,128)} async-done(((f32[1024,2048]{1,0:T(8,128)}), f32[256,2048]{1,0:T(8,128)}) %reduce-scatter.16.cloned.1.call-update) | async-done | bytes 2097168 | tf_op jit(solution)/shard_map/reduce_scatter | solution.py:248
  1138.1 149.2 %reduce-scatter.22.cloned.1.call-done = f32[128,2048]{1,0:T(8,128)} async-done(((f32[1024,2048]{1,0:T(8,128)}), f32[128,2048]{1,0:T(8,128)}) %reduce-scatter.22.cloned.1.call-update) | async-done | bytes 1048592 | tf_op jit(solution)/shard_map/reduce_scatter | solution.py:257
  1291.8 146.1 %reduce-scatter.18.cloned.1.call-done = f32[2,256,512]{2,1,0:T(8,128)} async-done(((f32[2,2048,512]{2,1,0:T(8,128)}), f32[2,256,512]{2,1,0:T(8,128)}) %reduce-scatter.18.cloned.1.call-update) | async-done | bytes 1048592 | tf_op jit(solution)/shard_map/reduce_scatter | solution.py:255
  1442.2 68.7 %reduce-scatter.12.cloned.1.call-done = f32[256,2048]{1,0:T(8,128)} async-done(((f32[1024,2048]{1,0:T(8,128)}), f32[256,2048]{1,0:T(8,128)}) %reduce-scatter.12.cloned.1.call-update) | async-done | bytes 2097168 | tf_op jit(solution)/shard_map/reduce_scatter | solution.py:204
  1510.9 5.9 fusion.42
  1516.9 277.7 %reduce-scatter.20.cloned.1.call-done = f32[2,256,1024]{2,1,0:T(8,128)} async-done(((f32[2,2048,1024]{2,1,0:T(8,128)}), f32[2,256,1024]{2,1,0:T(8,128)}) %reduce-scatter.20.cloned.1.call-update) | async-done | bytes 2097168 | tf_op jit(solution)/shard_map/reduce_scatter | solution.py:256
  1794.6 7.1 multiply_reduce_fusion.3
  1805.9 39.4 %all-reduce = (f32[2,2048]{1,0:T(2,128)S(1)}, f32[7]{0:T(128)S(1)}, f32[7]{0:T(128)S(1)}) all-reduce(f32[2,2048]{1,0:T(2,128)S(1)} %pad_maximum_fusion.4, f32[7]{0:T(128)S(1)} %concatenate.16, f32[7]{0:T(128)S(1)} %concatenate.15), channel_id=1, replica_groups=mesh['dp'=8,'mp'=4] {'dp','mp'}, use_global_device_ids=true, to_apply=%region_16.18 | all-reduce | flops 4110 | bytes 32880 | tf_op jit(solution)/shard_map/psum | solution.py:261
  (291 shorter events, 186.6 us)
Async XLA Ops:
  7.2 79.1 %all-gather.14.cloned.1.call-start = ((), (), s32[]{:S(2)}) async-start(), calls=%async_computation.11 | async-start | bytes 4718592 | tf_op jit(solution)/shard_map/all_gather | solution.py:153
  9.5 112.0 %all-gather.10.cloned.1.call-start = ((), (), s32[]{:S(2)}) async-start(), calls=%async_computation.9 | async-start | bytes 5242880 | tf_op jit(solution)/shard_map/all_gather | solution.py:174
  12.6 710.9 %copy-start.41 = (f32[1,2048]{1,0:T(1,128)}, f32[1,2048]{1,0:T(1,128)S(1)}, u32[]{:S(2)}) copy-start(f32[1,2048]{1,0:T(1,128)S(1)} %get-tuple-element.334) | copy-start | bytes 24580
  15.7 233.1 %all-gather.12.cloned.1.call-start = ((), (), s32[]{:S(2)}) async-start(), calls=%async_computation.10 | async-start | bytes 9437184 | tf_op jit(solution)/shard_map/all_gather | solution.py:154
  16.9 305.4 %all-gather.16.cloned.1.call-start = ((), (), s32[]{:S(2)}) async-start(), calls=%async_computation.12 | async-start | bytes 4718592 | tf_op jit(solution)/shard_map/all_gather | solution.py:155
  17.8 383.5 %reduce-scatter.10.cloned.1.call-start = ((), (), s32[]{:S(2)}) async-start(), calls=%async_computation.13 | async-start | bytes 10485760 | tf_op jit(solution)/shard_map/reduce_scatter | solution.py:193
  21.0 108.5 %copy-start.23 = (f32[1024,128]{0,1:T(8,128)}, f32[1024,128]{0,1:T(8,128)S(1)}, u32[]{:S(2)}) copy-start(f32[1024,128]{0,1:T(8,128)S(1)} %get-tuple-element.349) | copy-start | bytes 1572868
  102.0 24.9 %copy-start.39 = (bf16[2,128,2,2048]{3,2,1,0:T(2,128)(2,1)S(1)}, bf16[2,128,2,2048]{3,2,1,0:T(2,128)(2,1)}, u32[]{:S(2)}) copy-start(bf16[2,128,2,2048]{3,2,1,0:T(2,128)(2,1)} %dot_general.100) | copy-start | bytes 6291460
  316.8 14.4 copy-start.63
  331.2 70.1 %copy-start.3 = (bf16[256,2048]{1,0:T(8,128)(2,1)S(1)}, bf16[256,2048]{1,0:T(8,128)(2,1)}, u32[]{:S(2)}) copy-start(bf16[256,2048]{1,0:T(8,128)(2,1)} %param.26) | copy-start | bytes 3145732
  331.2 145.5 %all-gather.20.cloned.1.call-start = ((), (), s32[]{:S(2)}) async-start(), calls=%async_computation.15 | async-start | bytes 4718592 | tf_op jit(solution)/shard_map/all_gather | solution.py:156
  333.3 178.5 %all-gather.18.cloned.1.call-start = ((), (), s32[]{:S(2)}) async-start(), calls=%async_computation.14 | async-start | bytes 5242880 | tf_op jit(solution)/shard_map/all_gather | solution.py:201
  403.3 320.2 %copy-start = (f32[256,2048]{1,0:T(8,128)}, f32[256,2048]{1,0:T(8,128)S(1)}, u32[]{:S(2)}) copy-start(f32[256,2048]{1,0:T(8,128)S(1)} %get-tuple-element.310) | copy-start | bytes 6291460
  403.3 320.2 %copy-start.47 = (f32[256]{0:T(256)}, f32[256]{0:T(256)S(1)}, u32[]{:S(2)}) copy-start(f32[256]{0:T(256)S(1)} %fusion.62) | copy-start | bytes 3076
  404.8 143.1 %all-gather.24.cloned.1.call-start = ((), (), s32[]{:S(2)}) async-start(), calls=%async_computation.18 | async-start | bytes 5242880 | tf_op jit(solution)/shard_map/all_gather | solution.py:211
  405.6 217.9 %all-gather.22.cloned.1.call-start = ((), (), s32[]{:S(2)}) async-start(), calls=%async_computation.16 | async-start | bytes 4718592 | tf_op jit(solution)/shard_map/all_gather | solution.py:157
  407.7 312.9 %reduce-scatter.14.cloned.1.call-start = ((), (), s32[]{:S(2)}) async-start(), calls=%async_computation.19 | async-start | bytes 10485760 | tf_op jit(solution)/shard_map/reduce_scatter | solution.py:217
  623.4 20.2 %copy-start.62 = (bf16[2048,1024]{1,0:T(8,128)(2,1)S(1)}, bf16[2048,1024]{1,0:T(8,128)(2,1)}, u32[]{:S(2)}) copy-start(bf16[2048,1024]{1,0:T(8,128)(2,1)} %all-gather.20.cloned.1.call-done) | copy-start | bytes 12582916
  650.5 73.6 %copy-start.11 = (bf16[256,2048]{1,0:T(8,128)(2,1)S(1)}, bf16[256,2048]{1,0:T(8,128)(2,1)}, u32[]{:S(2)}) copy-start(bf16[256,2048]{1,0:T(8,128)(2,1)} %param.27) | copy-start | bytes 3145732
  650.5 109.9 %all-gather.26.cloned.1.call-start = ((), (), s32[]{:S(2)}) async-start(), calls=%async_computation.20 | async-start | bytes 5242880 | tf_op jit(solution)/shard_map/all_gather | solution.py:224
  725.8 232.9 %reduce-scatter.26.cloned.1.call-start = ((), (), s32[]{:S(2)}) async-start(), calls=%async_computation.26 | async-start | bytes 9437184 | tf_op jit(solution)/shard_map/reduce_scatter | solution.py:259
  739.1 323.7 %reduce-scatter.24.cloned.1.call-start = ((), (), s32[]{:S(2)}) async-start(), calls=%async_computation.25 | async-start | bytes 9437184 | tf_op jit(solution)/shard_map/reduce_scatter | solution.py:258
  749.7 386.0 %reduce-scatter.16.cloned.1.call-start = ((), (), s32[]{:S(2)}) async-start(), calls=%async_computation.21 | async-start | bytes 10485760 | tf_op jit(solution)/shard_map/reduce_scatter | solution.py:248
  760.4 11.2 copy-start.9
  760.4 11.2 copy-start.25
  875.9 12.2 copy-start.38
  875.9 12.2 slice-start
  907.3 380.0 %reduce-scatter.22.cloned.1.call-start = ((), (), s32[]{:S(2)}) async-start(), calls=%async_computation.24 | async-start | bytes 9437184 | tf_op jit(solution)/shard_map/reduce_scatter | solution.py:257
  917.9 520.0 %reduce-scatter.18.cloned.1.call-start = ((), (), s32[]{:S(2)}) async-start(), calls=%async_computation.22 | async-start | bytes 9437184 | tf_op jit(solution)/shard_map/reduce_scatter | solution.py:255
  929.7 581.2 %reduce-scatter.12.cloned.1.call-start = ((), (), s32[]{:S(2)}) async-start(), calls=%async_computation.17 | async-start | bytes 10485760 | tf_op jit(solution)/shard_map/reduce_scatter | solution.py:204
  940.3 854.4 %reduce-scatter.20.cloned.1.call-start = ((), (), s32[]{:S(2)}) async-start(), calls=%async_computation.23 | async-start | bytes 18874368 | tf_op jit(solution)/shard_map/reduce_scatter | solution.py:256
  958.7 104.1 %copy-start.15 = (f32[256,1024]{1,0:T(8,128)S(1)}, f32[256,1024]{1,0:T(8,128)}, u32[]{:S(2)}) copy-start(f32[256,1024]{1,0:T(8,128)} %param.32) | copy-start | bytes 3145732
  964.6 171.1 %copy-start.4 = (bf16[256,2048]{1,0:T(8,128)(2,1)S(1)}, bf16[256,2048]{1,0:T(8,128)(2,1)}, u32[]{:S(2)}) copy-start(bf16[256,2048]{1,0:T(8,128)(2,1)} %param.26) | copy-start | bytes 3145732
  964.6 171.1 %copy-start.45 = (f32[1,2048]{1,0:T(1,128)S(1)}, f32[1,2048]{1,0:T(1,128)}, u32[]{:S(2)}) copy-start(f32[1,2048]{1,0:T(1,128)} %copy-done.44) | copy-start | bytes 24580
  964.6 171.1 %copy-start.50 = (f32[256]{0:T(256)S(1)}, f32[256]{0:T(256)}, u32[]{:S(2)}) copy-start(f32[256]{0:T(256)} %copy-done.49) | copy-start | bytes 3076
  964.6 173.4 %copy-start.57 = (f32[256]{0:T(256)S(1)}, f32[256]{0:T(256)}, u32[]{:S(2)}) copy-start(f32[256]{0:T(256)} %copy-done.56) | copy-start | bytes 3076
  964.6 173.4 %copy-start.46 = (f32[2048]{0:T(1024)S(1)}, f32[2048]{0:T(1024)}, u32[]{:S(2)}) copy-start(f32[2048]{0:T(1024)} %get-tuple-element.232) | copy-start | bytes 24580
  964.7 322.6 %copy-start.18 = (f32[128,2048]{1,0:T(8,128)S(1)}, f32[128,2048]{1,0:T(8,128)}, u32[]{:S(2)}) copy-start(f32[128,2048]{1,0:T(8,128)} %param.31) | copy-start | bytes 3145732
  1291.8 219.1 %copy-start.1 = (f32[256,2048]{1,0:T(8,128)S(1)}, f32[256,2048]{1,0:T(8,128)}, u32[]{:S(2)}) copy-start(f32[256,2048]{1,0:T(8,128)} %copy-done) | copy-start | bytes 6291460
  1291.8 219.1 %copy-start.42 = (f32[1,2048]{1,0:T(1,128)S(1)}, f32[1,2048]{1,0:T(1,128)}, u32[]{:S(2)}) copy-start(f32[1,2048]{1,0:T(1,128)} %copy-done.41) | copy-start | bytes 24580
  1291.8 219.1 %copy-start.48 = (f32[256]{0:T(256)S(1)}, f32[256]{0:T(256)}, u32[]{:S(2)}) copy-start(f32[256]{0:T(256)} %copy-done.47) | copy-start | bytes 3076
  1291.8 219.1 %copy-start.55 = (f32[256]{0:T(256)S(1)}, f32[256]{0:T(256)}, u32[]{:S(2)}) copy-start(f32[256]{0:T(256)} %copy-done.54) | copy-start | bytes 3076
  1516.8 331.1 %copy-start.43 = (f32[2,2048]{1,0:T(2,128)S(1)}, f32[2,2048]{1,0:T(2,128)}, u32[]{:S(2)}) copy-start(f32[2,2048]{1,0:T(2,128)} %param.28) | copy-start | bytes 49156
  1516.8 331.1 %copy-start.51 = (f32[2,2048]{1,0:T(2,128)S(1)}, f32[2,2048]{1,0:T(2,128)}, u32[]{:S(2)}) copy-start(f32[2,2048]{1,0:T(2,128)} %param.35) | copy-start | bytes 49156
  1516.8 331.1 %copy-start.52 = (f32[2,2048]{1,0:T(2,128)S(1)}, f32[2,2048]{1,0:T(2,128)}, u32[]{:S(2)}) copy-start(f32[2,2048]{1,0:T(2,128)} %param.34) | copy-start | bytes 49156
  1516.8 333.4 %copy-start.13 = (f32[128,2048]{1,0:T(8,128)S(1)}, f32[128,2048]{1,0:T(8,128)}, u32[]{:S(2)}) copy-start(f32[128,2048]{1,0:T(8,128)} %param.33) | copy-start | bytes 3145732
  1516.8 333.4 %copy-start.26 = (f32[128,2048]{1,0:T(8,128)S(1)}, f32[128,2048]{1,0:T(8,128)}, u32[]{:S(2)}) copy-start(f32[128,2048]{1,0:T(8,128)} %get-tuple-element.297) | copy-start | bytes 3145732
  1801.7 51.5 %copy-start.16 = (f32[256,1024]{1,0:T(8,128)S(1)}, f32[256,1024]{1,0:T(8,128)}, u32[]{:S(2)}) copy-start(f32[256,1024]{1,0:T(8,128)} %param.32) | copy-start | bytes 3145732
  (39 other events, 157.3 us)
Sparse Core Ops, SparseCore 0:
  10.8 75.4 all-gather.13
  88.4 32.9 all-gather.9
  124.2 124.4 all-gather.11
  251.3 70.9 all-gather.15
  331.4 69.9 reduce-scatter.9
  403.9 72.7 all-gather.19
  478.8 32.9 all-gather.17
  513.4 34.4 all-gather.23
  550.6 72.7 all-gather.21
  650.6 69.9 reduce-scatter.13
  725.9 34.4 all-gather.25
  764.5 147.4 reduce-scatter.25
  916.2 146.5 reduce-scatter.23
  1065.2 70.4 reduce-scatter.15
  1139.8 147.4 reduce-scatter.21
  1291.3 146.5 reduce-scatter.17
  1440.3 70.5 reduce-scatter.11
  1515.1 279.4 reduce-scatter.19
where the time goes:
time: 1880 us; the launch traced here: 1870 us
  waiting for transfers between devices  1370 us (73%)
  matrix products  213 us (11%)
  local copies, waits for them, and re-layouts  129 us (7%)
  other arithmetic  99.3 us (5%)
  blocking collectives  39.4 us (2%)
    reduce_scatter x1, waiting for transfers between devices, body(): lax.psum_scatter(mixing_local, 'dp', scatter_dimension=1, tiled=True)  278 us
    reduce_scatter x1, waiting for transfers between devices, body(): lax.psum_scatter(output_local, 'dp', scatter_dimension=0, tiled=True)  149 us
    reduce_scatter x1, waiting for transfers between devices, body(): lax.psum_scatter(scoring_local, 'dp', scatter_dimension=1, tiled=True)  146 us
    all_gather x1, waiting for transfers between devices, body(): lax.all_gather(mixing_master.astype(jnp.bfloat16), 'dp', axis=1, tiled=True)  113 us
    reduce_scatter x1, waiting for transfers between devices, body(): lax.psum_scatter(expand_local, 'dp', scatter_dimension=0, tiled=True)  98.1 us
    all_gather x1, waiting for transfers between devices, body(): lax.all_gather(shrink_master.astype(jnp.bfloat16), 'dp', axis=0, tiled=True)  75.5 us
    reduce_scatter x1, waiting for transfers between devices, body(): lax.psum_scatter(contract_cols(upward_back, expand_low), 'mp', scatter_di...  70.1 us
    all_gather x1, waiting for transfers between devices, body(): lax.all_gather(expand_master.astype(jnp.bfloat16), 'dp', axis=0, tiled=True)  68.9 us
  transfers between devices with their start and end apart: 18, of which 17 were waited for; matrix products, arithmetic and copies ran while one was open for 19% of the time, Pallas kernels for 0%

commit v1 on v0

--- a/solution.py
+++ b/solution.py
@@ -11,6 +11,27 @@
 decay_rate = 0.01
 learn_rate = 0.5
 norm_epsilon = 1e-06
+
+
+def spread_clusters_on_mesh(local_block):
+    res = lax.axis_size("dp")
+    earlier = lax.axis_index("dp")
+    inbox = []
+    a_now, d_next, mixed_arr = (res, earlier, local_block.shape[1])
+    for k0 in [*range(a_now)]:
+        inbox.append((k0, (k0 + 1) % a_now))
+    next_value = jnp.zeros(
+        (*local_block.shape[:1], a_now * mixed_arr, *local_block.shape[2:]), local_block.dtype
+    )
+    field_out = local_block
+    for rr in tuple(range(a_now)):
+        near = (d_next - rr) % a_now
+        next_value = lax.dynamic_update_slice_in_dim(
+            next_value, field_out, near * mixed_arr, axis=1
+        )
+        if rr < a_now - 1:
+            field_out = lax.ppermute(field_out, "dp", inbox)
+    return next_value
 
 
 def rms_scale(values, gain_row):
@@ -150,7 +171,7 @@
     shrink_second,
 ):
     scoring_low, mixing_low, output_low, expand_low, shrink_low = (
-        lax.all_gather(scoring_master.astype(jnp.bfloat16), "dp", axis=1, tiled=True),
+        spread_clusters_on_mesh(scoring_master.astype(jnp.bfloat16)),
         lax.all_gather(mixing_master.astype(jnp.bfloat16), "dp", axis=1, tiled=True),
         lax.all_gather(output_master.astype(jnp.bfloat16), "dp", axis=0, tiled=True),
         lax.all_gather(expand_master.astype(jnp.bfloat16), "dp", axis=0, tiled=True),

time: 1880 us -> 1840 us (0.979)
  waiting for transfers between devices: 1370 us -> 1320 us
    ppermute x0 -> x7, waiting for transfers between devices: none -> 125 us  [spread_clusters_on_mesh(): field_out = lax.ppermute(field_out, 'dp', inbox)]
    all_gather x1, waiting for transfers between devices: 113 us -> 24.2 us  [body(): lax.all_gather(mixing_master.astype(jnp.bfloat16), 'dp', axis=1, tiled=True)]
    all_gather x1 -> x0, waiting for transfers between devices: 65.3 us -> none  [body(): lax.all_gather(scoring_master.astype(jnp.bfloat16), 'dp', axis=1, tiled=T...]
    all_gather x1, waiting for transfers between devices: 19.4 us -> 0.01 us  [body(): normed_all = lax.all_gather(normed, 'mp', axis=0, tiled=True)]
  transfers between devices with their start and end apart: 18 -> 24, of which waited for: 17 -> 22; matrix products, arithmetic and copies ran while one was open for 19% -> 20% of each run, Pallas kernels for 0% -> 0%
where the time goes in v1:
time: 1840 us; the launch traced here: 1830 us
  waiting for transfers between devices  1320 us (72%)
  matrix products  208 us (11%)
  local copies, waits for them, and re-layouts  142 us (8%)
  other arithmetic  99.1 us (5%)
  blocking collectives  39.4 us (2%)
    reduce_scatter x1, waiting for transfers between devices, body(): lax.psum_scatter(mixing_local, 'dp', scatter_dimension=1, tiled=True)  278 us
    reduce_scatter x1, waiting for transfers between devices, body(): lax.psum_scatter(output_local, 'dp', scatter_dimension=0, tiled=True)  149 us
    reduce_scatter x1, waiting for transfers between devices, body(): lax.psum_scatter(scoring_local, 'dp', scatter_dimension=1, tiled=True)  146 us
    ppermute x7, waiting for transfers between devices, spread_clusters_on_mesh(): field_out = lax.ppermute(field_out, 'dp', inbox)  125 us
    reduce_scatter x1, waiting for transfers between devices, body(): lax.psum_scatter(expand_local, 'dp', scatter_dimension=0, tiled=True)  102 us
    all_gather x1, waiting for transfers between devices, body(): lax.all_gather(shrink_master.astype(jnp.bfloat16), 'dp', axis=0, tiled=True)  75.5 us
    reduce_scatter x1, waiting for transfers between devices, body(): lax.psum_scatter(contract_cols(upward_back, expand_low), 'mp', scatter_di...  70 us
    all_gather x1, waiting for transfers between devices, body(): lax.all_gather(expand_master.astype(jnp.bfloat16), 'dp', axis=0, tiled=True)  69 us
  transfers between devices with their start and end apart: 24, of which 22 were waited for; matrix products, arithmetic and copies ran while one was open for 20% of the time, Pallas kernels for 0%

profile of v1, /device:TPU:0, one launch (start us, length us, event | category | flops | bytes accessed | tf_op | source)
XLA Modules:
  0.0 1834.9 jit_solution(15550542532874936303)
XLA Ops:
  18.6 15.0 collective-permute-done
  33.5 15.8 collective-permute-done.1
  50.1 14.1 collective-permute-done.2
  64.3 27.3 %collective-permute-done.3 = bf16[2,256,512]{2,1,0:T(8,128)(2,1)S(1)} collective-permute-done((bf16[2,256,512]{2,1,0:T(8,128)(2,1)S(1)}, bf16[2,256,512]{2,1,0:T(8,128)(2,1)S(1)}, u32[]{:S(2)}, u32[]{:S(2)}) %collective-permute-start.3) | collective-permute-done | bytes 524320 | tf_op jit(solution)/shard_map/ppermute | solution.py:33
  92.5 26.2 %collective-permute-done.4 = bf16[2,256,512]{2,1,0:T(8,128)(2,1)} collective-permute-done((bf16[2,256,512]{2,1,0:T(8,128)(2,1)S(1)}, bf16[2,256,512]{2,1,0:T(8,128)(2,1)}, u32[]{:S(2)}, u32[]{:S(2)}) %collective-permute-start.4) | collective-permute-done | bytes 524320 | tf_op jit(solution)/shard_map/ppermute | solution.py:33
  129.2 6.5 collective-permute-done.5
  143.2 20.4 %collective-permute-done.6 = bf16[2,256,512]{2,1,0:T(8,128)(2,1)S(1)} collective-permute-done((bf16[2,256,512]{2,1,0:T(8,128)(2,1)}, bf16[2,256,512]{2,1,0:T(8,128)(2,1)S(1)}, u32[]{:S(2)}, u32[]{:S(2)}) %collective-permute-start.6) | collective-permute-done | bytes 524320 | tf_op jit(solution)/shard_map/ppermute | solution.py:33
  190.1 24.2 %all-gather.11.cloned.1.call-done = bf16[2,2048,1024]{2,1,0:T(8,128)(2,1)} async-done(((bf16[2,256,1024]{2,1,0:T(8,128)(2,1)}), bf16[2,2048,1024]{2,1,0:T(8,128)(2,1)}) %all-gather.11.cloned.1.call-update) | async-done | bytes 8388624 | tf_op jit(solution)/shard_map/all_gather | solution.py:175
  214.3 8.0 fusion.51
  229.5 6.5 copy.92
  236.0 18.2 while.26
  254.2 7.3 copy.108
  261.5 7.0 reshape.309
  272.1 10.5 multiply_convert_fusion.4
  282.5 6.3 all-gather.13.cloned.1.call-done
  288.8 8.9 fusion.83
  299.9 68.0 %reduce-scatter.10.cloned.1.call-done = f32[256,2048]{1,0:T(8,128)} async-done(((f32[1024,2048]{1,0:T(8,128)}), f32[256,2048]{1,0:T(8,128)}) %reduce-scatter.10.cloned.1.call-update) | async-done | bytes 2097168 | tf_op jit(solution)/shard_map/reduce_scatter | solution.py:214
  374.2 69.0 %all-gather.17.cloned.1.call-done = bf16[2048,1024]{1,0:T(8,128)(2,1)} async-done(((bf16[256,1024]{1,0:T(8,128)(2,1)}), bf16[2048,1024]{1,0:T(8,128)(2,1)}) %all-gather.17.cloned.1.call-update) | async-done | bytes 4194320 | tf_op jit(solution)/shard_map/all_gather | solution.py:177
  443.2 35.0 %all-gather.15.cloned.1.call-done = bf16[1024,2048]{1,0:T(8,128)(2,1)} async-done(((bf16[256,2048]{1,0:T(8,128)(2,1)}), bf16[1024,2048]{1,0:T(8,128)(2,1)}) %all-gather.15.cloned.1.call-update) | async-done | bytes 4194320 | tf_op jit(solution)/shard_map/all_gather | solution.py:222
  478.2 10.1 fusion.84
  488.3 26.0 %all-gather.21.cloned.1.call-done = bf16[1024,2048]{1,0:T(8,128)(2,1)} async-done(((bf16[256,2048]{1,0:T(8,128)(2,1)}), bf16[1024,2048]{1,0:T(8,128)(2,1)}) %all-gather.21.cloned.1.call-update) | async-done | bytes 4194320 | tf_op jit(solution)/shard_map/all_gather | solution.py:232
  514.3 75.5 %all-gather.19.cloned.1.call-done = bf16[1024,2048]{1,0:T(8,128)(2,1)} async-done(((bf16[128,2048]{1,0:T(8,128)(2,1)}), bf16[1024,2048]{1,0:T(8,128)(2,1)}) %all-gather.19.cloned.1.call-update) | async-done | bytes 4194320 | tf_op jit(solution)/shard_map/all_gather | solution.py:178
  589.8 18.9 %add_convert_fusion = (bf16[1024,1024]{1,0:T(8,128)(2,1)S(1)}, f32[1024,1024]{1,0:T(8,128)}) fusion(f32[1024,1024]{1,0:T(8,128)} %fusion.84, bf16[1024,2048]{1,0:T(8,128)(2,1)} %all-gather.21.cloned.1.call-done, bf16[1024,2048]{1,0:T(8,128)(2,1)} %all-gather.19.cloned.1.call-done), kind=kOutput, calls=%fused_computation.54 | convolution fusion | flops 4370464768 | bytes 18874368 | tf_op jit(solution)/shard_map/dot_general | solution.py:86
  610.0 6.9 fusion.86
  616.9 70.0 %reduce-scatter.14.cloned.1.call-done = f32[256,2048]{1,0:T(8,128)} async-done(((f32[1024,2048]{1,0:T(8,128)}), f32[256,2048]{1,0:T(8,128)}) %reduce-scatter.14.cloned.1.call-update) | async-done | bytes 2097168 | tf_op jit(solution)/shard_map/reduce_scatter | solution.py:238
  698.3 7.2 fusion.89
  707.0 9.1 fusion.88
  716.2 10.6 all-gather.23.cloned.1.call-done
  726.7 11.1 multiply_reduce_fusion
  742.4 81.4 %while.27 = (s32[]{:T(128)}, f32[1024,2,256]{0,2,1:T(8,128)}, f32[1024,2,512]{0,2,1:T(8,128)}, f32[2,512,2,256]{1,0,3,2:T(2,128)}, s32[2]{0:T(128)S(1)}, /*index...) while((s32[]{:T(128)}, f32[1024,2,256]{0,2,1:T(8,128)}, ...), condition=%wide.region_11.13_spmd.clone, body=%wide.region_10.12_spmd.clone.sunk | while | flops 3772776960 | bytes 48765212 | solution.py:138
  755.2 6.8 bitcast_add_fusion.5
  762.0 19.6 %dynamic_update_slice.54 = f32[2,512,2,256]{1,0,3,2:T(2,128)} dynamic-update-slice(f32[2,512,2,256]{1,0,3,2:T(2,128)} %get-tuple-element.510, f32[1,512,2,256]{1,0,3,2:T(1,128)S(1)} %copy.180, s32[]{:T(128)S(6)} %copy.201, s32[]{:T(128)} %constant.93.clone.1..sunk.1, s32[]{:T(128)} %constant.93.clone.1..sunk.1, s32[]{:T(128)} %constant.93.clone.1..sunk.1) | dynamic-update-slice | bytes 2097156 | tf_op jit(solution)/shard_map/while/body/jit(dynamic_update_index_in_dim)/dynamic_update_slice | solution.py:138
  796.1 8.0 bitcast_add_fusion.5
  804.2 19.6 %dynamic_update_slice.54 = f32[2,512,2,256]{1,0,3,2:T(2,128)} dynamic-update-slice(f32[2,512,2,256]{1,0,3,2:T(2,128)} %get-tuple-element.510, f32[1,512,2,256]{1,0,3,2:T(1,128)S(1)} %copy.180, s32[]{:T(128)S(6)} %copy.201, s32[]{:T(128)} %constant.93.clone.1..sunk.1, s32[]{:T(128)} %constant.93.clone.1..sunk.1, s32[]{:T(128)} %constant.93.clone.1..sunk.1) | dynamic-update-slice | bytes 2097156 | tf_op jit(solution)/shard_map/while/body/jit(dynamic_update_index_in_dim)/dynamic_update_slice | solution.py:138
  851.6 6.8 fusion.34
  858.4 11.0 add_add_fusion
  871.1 9.0 fusion.87
  894.5 8.8 fusion.85
  903.4 7.2 convolution_bitcast_fusion.2
  915.3 6.3 pad_maximum_fusion
  927.5 101.6 %reduce-scatter.24.cloned.1.call-done = f32[256,1024]{1,0:T(8,128)} async-done(((f32[2048,1024]{1,0:T(8,128)}), f32[256,1024]{1,0:T(8,128)}) %reduce-scatter.24.cloned.1.call-update) | async-done | bytes 1048592 | tf_op jit(solution)/shard_map/reduce_scatter | solution.py:279
  1033.6 68.6 %reduce-scatter.16.cloned.1.call-done = f32[256,2048]{1,0:T(8,128)} async-done(((f32[1024,2048]{1,0:T(8,128)}), f32[256,2048]{1,0:T(8,128)}) %reduce-scatter.16.cloned.1.call-update) | async-done | bytes 2097168 | tf_op jit(solution)/shard_map/reduce_scatter | solution.py:269
  1104.5 149.2 %reduce-scatter.22.cloned.1.call-done = f32[128,2048]{1,0:T(8,128)} async-done(((f32[1024,2048]{1,0:T(8,128)}), f32[128,2048]{1,0:T(8,128)}) %reduce-scatter.22.cloned.1.call-update) | async-done | bytes 1048592 | tf_op jit(solution)/shard_map/reduce_scatter | solution.py:278
  1258.3 146.1 %reduce-scatter.18.cloned.1.call-done = f32[2,256,512]{2,1,0:T(8,128)} async-done(((f32[2,2048,512]{2,1,0:T(8,128)}), f32[2,256,512]{2,1,0:T(8,128)}) %reduce-scatter.18.cloned.1.call-update) | async-done | bytes 1048592 | tf_op jit(solution)/shard_map/reduce_scatter | solution.py:276
  1408.7 68.7 %reduce-scatter.12.cloned.1.call-done = f32[256,2048]{1,0:T(8,128)} async-done(((f32[1024,2048]{1,0:T(8,128)}), f32[256,2048]{1,0:T(8,128)}) %reduce-scatter.12.cloned.1.call-update) | async-done | bytes 2097168 | tf_op jit(solution)/shard_map/reduce_scatter | solution.py:225
  1483.3 277.8 %reduce-scatter.20.cloned.1.call-done = f32[2,256,1024]{2,1,0:T(8,128)} async-done(((f32[2,2048,1024]{2,1,0:T(8,128)}), f32[2,256,1024]{2,1,0:T(8,128)}) %reduce-scatter.20.cloned.1.call-update) | async-done | bytes 2097168 | tf_op jit(solution)/shard_map/reduce_scatter | solution.py:277
  1761.1 7.1 multiply_reduce_fusion.3
  1772.4 39.4 %all-reduce = (f32[2,2048]{1,0:T(2,128)S(1)}, f32[7]{0:T(128)S(1)}, f32[7]{0:T(128)S(1)}) all-reduce(f32[2,2048]{1,0:T(2,128)S(1)} %pad_maximum_fusion.4, f32[7]{0:T(128)S(1)} %concatenate.16, f32[7]{0:T(128)S(1)} %concatenate.15), channel_id=1, replica_groups=mesh['dp'=8,'mp'=4] {'dp','mp'}, use_global_device_ids=true, to_apply=%region_16.18 | all-reduce | flops 4110 | bytes 32880 | tf_op jit(solution)/shard_map/psum | solution.py:282
  (325 shorter events, 231.7 us)
Async XLA Ops:
  7.2 168.5 %all-gather.9.cloned.1.call-start = ((), (), s32[]{:S(2)}) async-start(), calls=%async_computation.9 | async-start | bytes 5242880 | tf_op jit(solution)/shard_map/all_gather | solution.py:195
  9.8 680.0 %copy-start.44 = (f32[1,2048]{1,0:T(1,128)}, f32[1,2048]{1,0:T(1,128)S(1)}, u32[]{:S(2)}) copy-start(f32[1,2048]{1,0:T(1,128)S(1)} %get-tuple-element.334) | copy-start | bytes 24580
  10.4 81.2 %copy-start.16 = (f32[128,2048]{1,0:T(8,128)S(1)}, f32[128,2048]{1,0:T(8,128)}, u32[]{:S(2)}) copy-start(f32[128,2048]{1,0:T(8,128)} %param.31) | copy-start | bytes 3145732
  13.0 201.4 %all-gather.11.cloned.1.call-start = ((), (), s32[]{:S(2)}) async-start(), calls=%async_computation.10 | async-start | bytes 9437184 | tf_op jit(solution)/shard_map/all_gather | solution.py:175
  14.2 274.6 %all-gather.13.cloned.1.call-start = ((), (), s32[]{:S(2)}) async-start(), calls=%async_computation.11 | async-start | bytes 4718592 | tf_op jit(solution)/shard_map/all_gather | solution.py:176
  15.5 18.0 collective-permute-start
  33.5 85.4 %copy-start.42 = (bf16[2,256,512]{2,1,0:T(8,128)(2,1)}, bf16[2,256,512]{2,1,0:T(8,128)(2,1)S(1)}, u32[]{:S(2)}) copy-start(bf16[2,256,512]{2,1,0:T(8,128)(2,1)S(1)} %collective-permute-done) | copy-start | bytes 1572868
  33.5 15.8 collective-permute-start.1
  49.3 14.9 collective-permute-start.2
  64.2 27.3 %collective-permute-start.3 = (bf16[2,256,512]{2,1,0:T(8,128)(2,1)S(1)}, bf16[2,256,512]{2,1,0:T(8,128)(2,1)S(1)}, u32[]{:S(2)}, u32[]{:S(2)}) collective-permute-start(bf16[2,256,512]{2,1,0:T(8,128)(2,1)S(1)} %collective-permute-done.2), channel_id=1, source_target_pairs={{0,4},{4,8},{8,12},{12,16},{16,20},{20,24},{24,28},{28,0},{1,5},{5... | collective-permute-start | bytes 1572872 | tf_op jit(solution)/shard_map/ppermute | solution.py:33
  91.6 27.2 %collective-permute-start.4 = (bf16[2,256,512]{2,1,0:T(8,128)(2,1)S(1)}, bf16[2,256,512]{2,1,0:T(8,128)(2,1)}, u32[]{:S(2)}, u32[]{:S(2)}) collective-permute-start(bf16[2,256,512]{2,1,0:T(8,128)(2,1)S(1)} %collective-permute-done.3), channel_id=1, source_target_pairs={{0,4},{4,8},{8,12},{12,16},{16,20},{20,24},{24,28},{28,0},{1,5},{5... | collective-permute-start | bytes 1572872 | tf_op jit(solution)/shard_map/ppermute | solution.py:33
  92.5 275.4 %reduce-scatter.10.cloned.1.call-start = ((), (), s32[]{:S(2)}) async-start(), calls=%async_computation.12 | async-start | bytes 10485760 | tf_op jit(solution)/shard_map/reduce_scatter | solution.py:214
  118.8 17.0 collective-permute-start.5
  125.6 58.0 %copy-start.22 = (f32[1024,128]{0,1:T(8,128)}, f32[1024,128]{0,1:T(8,128)S(1)}, u32[]{:S(2)}) copy-start(f32[1024,128]{0,1:T(8,128)S(1)} %get-tuple-element.349) | copy-start | bytes 1572868
  135.7 27.9 %collective-permute-start.6 = (bf16[2,256,512]{2,1,0:T(8,128)(2,1)}, bf16[2,256,512]{2,1,0:T(8,128)(2,1)S(1)}, u32[]{:S(2)}, u32[]{:S(2)}) collective-permute-start(bf16[2,256,512]{2,1,0:T(8,128)(2,1)} %collective-permute-done.5), channel_id=1, source_target_pairs={{0,4},{4,8},{8,12},{12,16},{16,20},{20,24},{24,28},{28,0},{1,5},{5... | collective-permute-start | bytes 1572872 | tf_op jit(solution)/shard_map/ppermute | solution.py:33
  297.7 70.1 %copy-start.3 = (bf16[256,2048]{1,0:T(8,128)(2,1)S(1)}, bf16[256,2048]{1,0:T(8,128)(2,1)}, u32[]{:S(2)}) copy-start(bf16[256,2048]{1,0:T(8,128)(2,1)} %param.26) | copy-start | bytes 3145732
  297.8 145.5 %all-gather.17.cloned.1.call-start = ((), (), s32[]{:S(2)}) async-start(), calls=%async_computation.14 | async-start | bytes 4718592 | tf_op jit(solution)/shard_map/all_gather | solution.py:177
  299.9 178.4 %all-gather.15.cloned.1.call-start = ((), (), s32[]{:S(2)}) async-start(), calls=%async_computation.13 | async-start | bytes 5242880 | tf_op jit(solution)/shard_map/all_gather | solution.py:222
  369.8 320.0 %copy-start = (f32[256,2048]{1,0:T(8,128)}, f32[256,2048]{1,0:T(8,128)S(1)}, u32[]{:S(2)}) copy-start(f32[256,2048]{1,0:T(8,128)S(1)} %get-tuple-element.310) | copy-start | bytes 6291460
  369.8 320.0 %copy-start.50 = (f32[256]{0:T(256)}, f32[256]{0:T(256)S(1)}, u32[]{:S(2)}) copy-start(f32[256]{0:T(256)S(1)} %fusion.62) | copy-start | bytes 3076
  371.3 143.0 %all-gather.21.cloned.1.call-start = ((), (), s32[]{:S(2)}) async-start(), calls=%async_computation.17 | async-start | bytes 5242880 | tf_op jit(solution)/shard_map/all_gather | solution.py:232
  372.0 217.8 %all-gather.19.cloned.1.call-start = ((), (), s32[]{:S(2)}) async-start(), calls=%async_computation.15 | async-start | bytes 4718592 | tf_op jit(solution)/shard_map/all_gather | solution.py:178
  374.2 312.8 %reduce-scatter.14.cloned.1.call-start = ((), (), s32[]{:S(2)}) async-start(), calls=%async_computation.18 | async-start | bytes 10485760 | tf_op jit(solution)/shard_map/reduce_scatter | solution.py:238
  616.9 73.5 %copy-start.10 = (bf16[256,2048]{1,0:T(8,128)(2,1)S(1)}, bf16[256,2048]{1,0:T(8,128)(2,1)}, u32[]{:S(2)}) copy-start(bf16[256,2048]{1,0:T(8,128)(2,1)} %param.27) | copy-start | bytes 3145732
  616.9 109.9 %all-gather.23.cloned.1.call-start = ((), (), s32[]{:S(2)}) async-start(), calls=%async_computation.19 | async-start | bytes 5242880 | tf_op jit(solution)/shard_map/all_gather | solution.py:245
  692.1 229.6 %reduce-scatter.26.cloned.1.call-start = ((), (), s32[]{:S(2)}) async-start(), calls=%async_computation.25 | async-start | bytes 9437184 | tf_op jit(solution)/shard_map/reduce_scatter | solution.py:280
  705.5 323.6 %reduce-scatter.24.cloned.1.call-start = ((), (), s32[]{:S(2)}) async-start(), calls=%async_computation.24 | async-start | bytes 9437184 | tf_op jit(solution)/shard_map/reduce_scatter | solution.py:279
  716.1 386.1 %reduce-scatter.16.cloned.1.call-start = ((), (), s32[]{:S(2)}) async-start(), calls=%async_computation.20 | async-start | bytes 10485760 | tf_op jit(solution)/shard_map/reduce_scatter | solution.py:269
  869.5 384.3 %reduce-scatter.22.cloned.1.call-start = ((), (), s32[]{:S(2)}) async-start(), calls=%async_computation.23 | async-start | bytes 9437184 | tf_op jit(solution)/shard_map/reduce_scatter | solution.py:278
  880.1 524.3 %reduce-scatter.18.cloned.1.call-start = ((), (), s32[]{:S(2)}) async-start(), calls=%async_computation.21 | async-start | bytes 9437184 | tf_op jit(solution)/shard_map/reduce_scatter | solution.py:276
  892.9 584.5 %reduce-scatter.12.cloned.1.call-start = ((), (), s32[]{:S(2)}) async-start(), calls=%async_computation.16 | async-start | bytes 10485760 | tf_op jit(solution)/shard_map/reduce_scatter | solution.py:225
  903.3 857.8 %reduce-scatter.20.cloned.1.call-start = ((), (), s32[]{:S(2)}) async-start(), calls=%async_computation.22 | async-start | bytes 18874368 | tf_op jit(solution)/shard_map/reduce_scatter | solution.py:277
  921.7 107.4 %copy-start.14 = (f32[256,1024]{1,0:T(8,128)S(1)}, f32[256,1024]{1,0:T(8,128)}, u32[]{:S(2)}) copy-start(f32[256,1024]{1,0:T(8,128)} %param.32) | copy-start | bytes 3145732
  927.5 174.8 %copy-start.4 = (bf16[256,2048]{1,0:T(8,128)(2,1)S(1)}, bf16[256,2048]{1,0:T(8,128)(2,1)}, u32[]{:S(2)}) copy-start(bf16[256,2048]{1,0:T(8,128)(2,1)} %param.26) | copy-start | bytes 3145732
  927.5 174.8 %copy-start.48 = (f32[1,2048]{1,0:T(1,128)S(1)}, f32[1,2048]{1,0:T(1,128)}, u32[]{:S(2)}) copy-start(f32[1,2048]{1,0:T(1,128)} %copy-done.47) | copy-start | bytes 24580
  927.5 174.8 %copy-start.53 = (f32[256]{0:T(256)S(1)}, f32[256]{0:T(256)}, u32[]{:S(2)}) copy-start(f32[256]{0:T(256)} %copy-done.52) | copy-start | bytes 3076
  927.5 177.0 %copy-start.60 = (f32[256]{0:T(256)S(1)}, f32[256]{0:T(256)}, u32[]{:S(2)}) copy-start(f32[256]{0:T(256)} %copy-done.59) | copy-start | bytes 3076
  927.5 177.1 %copy-start.49 = (f32[2048]{0:T(1024)S(1)}, f32[2048]{0:T(1024)}, u32[]{:S(2)}) copy-start(f32[2048]{0:T(1024)} %get-tuple-element.232) | copy-start | bytes 24580
  927.5 326.3 %copy-start.17 = (f32[128,2048]{1,0:T(8,128)S(1)}, f32[128,2048]{1,0:T(8,128)}, u32[]{:S(2)}) copy-start(f32[128,2048]{1,0:T(8,128)} %param.31) | copy-start | bytes 3145732
  1258.3 219.1 %copy-start.1 = (f32[256,2048]{1,0:T(8,128)S(1)}, f32[256,2048]{1,0:T(8,128)}, u32[]{:S(2)}) copy-start(f32[256,2048]{1,0:T(8,128)} %copy-done) | copy-start | bytes 6291460
  1258.3 219.1 %copy-start.45 = (f32[1,2048]{1,0:T(1,128)S(1)}, f32[1,2048]{1,0:T(1,128)}, u32[]{:S(2)}) copy-start(f32[1,2048]{1,0:T(1,128)} %copy-done.44) | copy-start | bytes 24580
  1258.3 219.1 %copy-start.51 = (f32[256]{0:T(256)S(1)}, f32[256]{0:T(256)}, u32[]{:S(2)}) copy-start(f32[256]{0:T(256)} %copy-done.50) | copy-start | bytes 3076
  1258.3 219.1 %copy-start.58 = (f32[256]{0:T(256)S(1)}, f32[256]{0:T(256)}, u32[]{:S(2)}) copy-start(f32[256]{0:T(256)} %copy-done.57) | copy-start | bytes 3076
  1483.3 331.2 %copy-start.46 = (f32[2,2048]{1,0:T(2,128)S(1)}, f32[2,2048]{1,0:T(2,128)}, u32[]{:S(2)}) copy-start(f32[2,2048]{1,0:T(2,128)} %param.28) | copy-start | bytes 49156
  1483.3 331.2 %copy-start.54 = (f32[2,2048]{1,0:T(2,128)S(1)}, f32[2,2048]{1,0:T(2,128)}, u32[]{:S(2)}) copy-start(f32[2,2048]{1,0:T(2,128)} %param.35) | copy-start | bytes 49156
  1483.3 331.2 %copy-start.55 = (f32[2,2048]{1,0:T(2,128)S(1)}, f32[2,2048]{1,0:T(2,128)}, u32[]{:S(2)}) copy-start(f32[2,2048]{1,0:T(2,128)} %param.34) | copy-start | bytes 49156
  1483.3 333.4 %copy-start.12 = (f32[128,2048]{1,0:T(8,128)S(1)}, f32[128,2048]{1,0:T(8,128)}, u32[]{:S(2)}) copy-start(f32[128,2048]{1,0:T(8,128)} %param.33) | copy-start | bytes 3145732
  1483.3 333.4 %copy-start.25 = (f32[128,2048]{1,0:T(8,128)S(1)}, f32[128,2048]{1,0:T(8,128)}, u32[]{:S(2)}) copy-start(f32[128,2048]{1,0:T(8,128)} %get-tuple-element.297) | copy-start | bytes 3145732
  (49 other events, 285.5 us)
Sparse Core Ops, SparseCore 0:
  13.1 37.1 all-gather.8
  53.1 161.2 all-gather.10
  217.0 71.7 all-gather.12
  297.9 69.9 reduce-scatter.9
  370.4 72.7 all-gather.16
  445.2 32.9 all-gather.14
  479.8 34.4 all-gather.20
  517.0 72.7 all-gather.18
  617.0 69.9 reduce-scatter.13
  692.2 34.4 all-gather.22
  730.9 147.4 reduce-scatter.25
  882.5 146.5 reduce-scatter.23
  1031.6 70.5 reduce-scatter.15
  1106.3 147.4 reduce-scatter.21
  1257.8 146.5 reduce-scatter.17
  1406.8 70.4 reduce-scatter.11
  1481.5 279.5 reduce-scatter.19
